TPU v7x, 32 devices: a whole 2x2x4 slice. The times are simulated.
32 devices in a mesh: shards: 4 (over x, core), context: 2 (over y), tensor: 4 (over z).
Axes of the slice: x: 2, y: 2, z: 4, core: 2. Of those that a mesh axis runs over, the one named last changes fastest.
Arguments:
- tokens: bfloat16 [8192, 1280], P(('shards', 'context')), may hold values from -6 to 6
- cotangent: bfloat16 [8192, 1280], P(('shards', 'context')), may hold values from -6 to 6
- segments: int32 [8192], P(('shards', 'context')), may hold values from 0 to 1024, as said below
- positions: int32 [8192], P(('shards', 'context')), may hold values from 0 to 1279, as said below
- w_query: bfloat16 [1280, 1280], P('shards', 'tensor'), may hold values from -0.15625 to 0.15625
- w_key: bfloat16 [1280, 1280], P('shards', 'tensor'), may hold values from -0.15625 to 0.15625
- w_value: bfloat16 [1280, 1280], P('shards', 'tensor'), may hold values from -0.15625 to 0.15625
- w_output: bfloat16 [1280, 1280], P('tensor', 'shards'), may hold values from -0.15625 to 0.15625
- w_up: bfloat16 [1280, 5120], P('shards', 'tensor'), may hold values from -0.15625 to 0.15625
- w_gate: bfloat16 [1280, 5120], P('shards', 'tensor'), may hold values from -0.15625 to 0.15625
- w_down: bfloat16 [5120, 1280], P('tensor', 'shards'), may hold values from -0.078125 to 0.078125
- scale_qk: float32 [1280], P('tensor'), may hold values from 1 to 1.6
- alpha_attn: float32 [1280], replicated, may hold values from 0.15 to 0.6
- alpha_mlp: float32 [1280], replicated, may hold values from 0.15 to 0.6
- scale_up: float32 [5120], P('tensor'), may hold values from 0.25 to 1.75
- scale_gate: float32 [5120], P('tensor'), may hold values from 0.25 to 1.75
Outputs:
- block_out: bfloat16 [8192, 1280], P(('shards', 'context'))
- grad_tokens: bfloat16 [8192, 1280], P(('shards', 'context'))
- grad_query: float32 [1280, 1280], P('shards', 'tensor')
- grad_key: float32 [1280, 1280], P('shards', 'tensor')
- grad_value: float32 [1280, 1280], P('shards', 'tensor')
- grad_output: float32 [1280, 1280], P('tensor', 'shards')
- grad_up: float32 [1280, 5120], P('shards', 'tensor')
- grad_gate: float32 [1280, 5120], P('shards', 'tensor')
- grad_down: float32 [5120, 1280], P('tensor', 'shards')
- grad_scale_qk: float32 [1280], P('tensor')
- grad_alpha_attn: float32 [1280], replicated
- grad_alpha_mlp: float32 [1280], replicated
- grad_scale_up: float32 [5120], P('tensor')
- grad_scale_gate: float32 [5120], P('tensor')
Inputs may be any that keep to these rules, and one draw needn't show every extreme that they name: `segments`: each run of 1024 tokens in order (one device of shards and context) holds first 512 prompt tokens (id 0), the prompt's tokens lying in order over the group, then 512 slots filled with whole continuations of 1 to 256 tokens each, one of exactly 256; a continuation's tokens are consecutive and its id is shared by no other continuation of the group. `positions`: A prompt token's position is its index in the group's prompt; a continuation token's is 1024 plus its offset in its continuation.
All inputs are finite; a program needn't handle non-finite values.
Results may differ from a plain program's by a relative error of at most 0.02.
Values may be sent and summed in bfloat16 or wider, within the bound.
No kernel may reach another device: no remote copies, remote signals or barrier semaphores. Data moves between devices by JAX's collectives and lax.ppermute only.
A program may use at most 192 MiB of HBM per device.

v0:
```python
import math
import jax
import jax.numpy as jnp
from jax import lax
from jax.sharding import PartitionSpec as P

HD = 64
CONT_DEV = 2
CONT_LEN = 256
EPSILON = 1e-06
MASKED = -1e30


def renorm(vector):
    return vector * lax.rsqrt(jnp.mean(vector * vector, axis=-1, keepdims=True) + EPSILON)


def rotate(values, cosine_table, sine_table):
    half_size = values.shape[-1] // 2
    first_half = values[..., :half_size]
    second_half = values[..., half_size:]
    return jnp.concatenate(
        [
            first_half * cosine_table - second_half * sine_table,
            second_half * cosine_table + first_half * sine_table,
        ],
        axis=-1,
    )


def head_norm(raw_heads, cosine_table, sine_table, factor):
    turned = rotate(raw_heads, cosine_table[:, None, :], sine_table[:, None, :])
    return factor * turned * lax.rsqrt(jnp.sum(turned * turned, axis=-1, keepdims=True) + EPSILON)


def residual_step(hidden, branch, alpha):
    return renorm(hidden + alpha * (renorm(branch) - hidden))


def swiglu(up_proj, gate_proj, scale_up, scale_gate):
    return scale_up * up_proj * jax.nn.silu(scale_gate * gate_proj)


def phase_tables(positions, head_size):
    half_size = head_size // 2
    frequency = 10000.0 ** (-(jnp.arange(half_size, dtype=jnp.float32) * 2.0 / head_size))
    phases = positions.astype(jnp.float32)[:, None] * frequency[None, :]
    return (jnp.cos(phases), jnp.sin(phases))


def outer_sum(left, right):
    return lax.dot_general(
        left, right, (((0,), (0,)), ((), ())), preferred_element_type=jnp.float32
    )


def back_product(gradient, weight):
    return lax.dot_general(
        gradient, weight, (((1,), (1,)), ((), ())), preferred_element_type=jnp.float32
    )


def to_heads(flat, head_size):
    return jnp.swapaxes(flat.reshape(flat.shape[0], -1, head_size), 0, 1)


def from_heads(stacked):
    return jnp.swapaxes(stacked, 0, 1).reshape(stacked.shape[1], -1)


def on_device(
    tokens,
    cotangent,
    segments,
    positions,
    w_query,
    w_key,
    w_value,
    w_output,
    w_up,
    w_gate,
    w_down,
    scale_qk,
    alpha_attn,
    alpha_mlp,
    scale_up,
    scale_gate,
):
    full_query, full_key, full_value, full_output, full_up, full_gate, full_down = (
        lax.all_gather(w_query, "shards", axis=0, tiled=True),
        lax.all_gather(w_key, "shards", axis=0, tiled=True),
        lax.all_gather(w_value, "shards", axis=0, tiled=True),
        lax.all_gather(w_output, "shards", axis=1, tiled=True),
        lax.all_gather(w_up, "shards", axis=0, tiled=True),
        lax.all_gather(w_gate, "shards", axis=0, tiled=True),
        lax.all_gather(w_down, "shards", axis=1, tiled=True),
    )
    row_count = tokens.shape[0]
    prompt_rows = row_count - CONT_DEV * CONT_LEN
    heads_local = scale_qk.shape[0] // HD
    multiplier = math.sqrt(HD)
    factor = scale_qk.reshape(heads_local, HD)
    cosine_table, sine_table = phase_tables(positions, HD)

    def normalize(raw_heads, factor_heads):
        return head_norm(raw_heads, cosine_table, sine_table, factor_heads)

    query_raw = jnp.dot(tokens, full_query, preferred_element_type=jnp.float32).reshape(
        row_count, heads_local, HD
    )
    key_raw = jnp.dot(tokens, full_key, preferred_element_type=jnp.float32).reshape(
        row_count, heads_local, HD
    )
    value_low = jnp.dot(tokens, full_value, preferred_element_type=jnp.float32).astype(jnp.bfloat16)
    query_normed, query_back = jax.vjp(normalize, query_raw, factor)
    key_normed, key_back = jax.vjp(normalize, key_raw, factor)
    query_low = query_normed.astype(jnp.bfloat16).reshape(row_count, -1)
    key_low = key_normed.astype(jnp.bfloat16).reshape(row_count, -1)
    prompt_keys, prompt_values = (
        lax.all_gather(key_low[:prompt_rows], "context", axis=0, tiled=True),
        lax.all_gather(value_low[:prompt_rows], "context", axis=0, tiled=True),
    )
    prompt_total = prompt_keys.shape[0]
    key_positions = jnp.concatenate(
        [jnp.arange(prompt_total, dtype=jnp.int32), positions[prompt_rows:]]
    )
    key_segments = jnp.concatenate([jnp.zeros((prompt_total,), jnp.int32), segments[prompt_rows:]])
    allowed = (key_positions[None, :] <= positions[:, None]) & (
        (key_segments[None, :] == 0) | (key_segments[None, :] == segments[:, None])
    )
    key_heads = to_heads(jnp.concatenate([prompt_keys, key_low[prompt_rows:]], axis=0), HD)
    value_heads = to_heads(jnp.concatenate([prompt_values, value_low[prompt_rows:]], axis=0), HD)
    key_heads, value_heads = (key_heads, value_heads)
    query_heads = to_heads(query_low, HD)

    def masked_scores(query_head, key_head):
        scores = multiplier * jnp.einsum(
            "qd,kd->qk", query_head, key_head, preferred_element_type=jnp.float32
        )
        return jnp.where(allowed, scores, MASKED)

    def attend_head(operands):
        query_head, key_head, value_head = operands
        scores = masked_scores(query_head, key_head)
        row_peak = jnp.max(scores, axis=1, keepdims=True)
        weights = jnp.exp(scores - row_peak)
        row_total = jnp.sum(weights, axis=1, keepdims=True)
        softmax_low = (weights / row_total).astype(jnp.bfloat16)
        head_out = jnp.dot(softmax_low, value_head, preferred_element_type=jnp.float32).astype(
            jnp.bfloat16
        )
        return (head_out, (row_peak + jnp.log(row_total))[:, 0])

    mixed_heads, log_totals = lax.map(attend_head, (query_heads, key_heads, value_heads))
    mixed_low = from_heads(mixed_heads)
    attn_terms = jnp.dot(mixed_low, full_output, preferred_element_type=jnp.float32)
    attn_out = lax.psum(attn_terms, "tensor")
    after_attn, attn_back = jax.vjp(residual_step, tokens.astype(jnp.float32), attn_out, alpha_attn)
    after_low = after_attn.astype(jnp.bfloat16)
    up_proj = jnp.dot(after_low, full_up, preferred_element_type=jnp.float32)
    gate_proj = jnp.dot(after_low, full_gate, preferred_element_type=jnp.float32)
    inner, swiglu_back = jax.vjp(swiglu, up_proj, gate_proj, scale_up, scale_gate)
    inner_low = inner.astype(jnp.bfloat16)
    merged_terms = jnp.dot(inner_low, full_down, preferred_element_type=jnp.float32)
    merged = lax.psum(merged_terms, "tensor")
    block_whole, out_back = jax.vjp(residual_step, after_attn, merged, alpha_mlp)
    block_low = block_whole.astype(jnp.bfloat16)
    grad_after, grad_merged, grad_alpha_mlp = out_back(cotangent.astype(jnp.float32))
    merged_grad_low = grad_merged.astype(jnp.bfloat16)
    grad_down = outer_sum(inner_low, merged_grad_low)
    grad_up_proj, grad_gate_proj, grad_scale_up, grad_scale_gate = swiglu_back(
        back_product(merged_grad_low, full_down)
    )
    up_grad_low = grad_up_proj.astype(jnp.bfloat16)
    gate_grad_low = grad_gate_proj.astype(jnp.bfloat16)
    grad_up = outer_sum(after_low, up_grad_low)
    grad_gate = outer_sum(after_low, gate_grad_low)
    input_terms = back_product(up_grad_low, full_up) + back_product(gate_grad_low, full_gate)
    grad_after = grad_after + lax.psum(input_terms, "tensor")
    grad_tokens_direct, grad_attn, grad_alpha_attn = attn_back(grad_after)
    attn_grad_low = grad_attn.astype(jnp.bfloat16)
    grad_output = outer_sum(mixed_low, attn_grad_low)
    grad_mixed_heads = to_heads(back_product(attn_grad_low, full_output).astype(jnp.bfloat16), HD)
    back_keys, back_values = (key_heads, value_heads)

    def head_backward(operands):
        query_head, key_head, value_head, grad_head, log_total = operands
        softmax_full = jnp.exp(masked_scores(query_head, key_head) - log_total[:, None])
        grad_softmax = jnp.einsum(
            "qd,kd->qk", grad_head, value_head, preferred_element_type=jnp.float32
        )
        weighted = jnp.sum(softmax_full * grad_softmax, axis=1, keepdims=True)
        grad_scores = (softmax_full * (grad_softmax - weighted)).astype(jnp.bfloat16)
        grad_query_head = multiplier * jnp.dot(
            grad_scores, key_head, preferred_element_type=jnp.float32
        )
        grad_key_head = multiplier * outer_sum(grad_scores, query_head)
        grad_value_head = outer_sum(softmax_full.astype(jnp.bfloat16), grad_head)
        return (grad_query_head, grad_key_head, grad_value_head)

    grad_query_heads, grad_key_heads, grad_value_heads = lax.map(
        head_backward, (query_heads, back_keys, back_values, grad_mixed_heads, log_totals)
    )
    grad_key_flat = from_heads(grad_key_heads)
    grad_value_flat = from_heads(grad_value_heads)
    prompt_grad_keys, prompt_grad_values = (
        lax.psum_scatter(
            grad_key_flat[:prompt_total].astype(jnp.bfloat16),
            "context",
            scatter_dimension=0,
            tiled=True,
        ).astype(jnp.float32),
        lax.psum_scatter(
            grad_value_flat[:prompt_total].astype(jnp.bfloat16),
            "context",
            scatter_dimension=0,
            tiled=True,
        ).astype(jnp.float32),
    )
    grad_key_rows = jnp.concatenate([prompt_grad_keys, grad_key_flat[prompt_total:]], axis=0)
    grad_value_rows = jnp.concatenate([prompt_grad_values, grad_value_flat[prompt_total:]], axis=0)
    grad_query_raw, grad_factor_query = query_back(
        from_heads(grad_query_heads).reshape(row_count, heads_local, HD)
    )
    grad_key_raw, grad_factor_key = key_back(grad_key_rows.reshape(row_count, heads_local, HD))
    query_grad_low = grad_query_raw.reshape(row_count, -1).astype(jnp.bfloat16)
    key_grad_low = grad_key_raw.reshape(row_count, -1).astype(jnp.bfloat16)
    value_grad_low = grad_value_rows.astype(jnp.bfloat16)
    grad_query = outer_sum(tokens, query_grad_low)
    grad_key = outer_sum(tokens, key_grad_low)
    grad_value = outer_sum(tokens, value_grad_low)
    token_terms = (
        back_product(query_grad_low, full_query)
        + back_product(key_grad_low, full_key)
        + back_product(value_grad_low, full_value)
    )
    grad_tokens = (
        grad_tokens_direct
        + lax.psum(token_terms.astype(jnp.bfloat16), "tensor").astype(jnp.float32)
    ).astype(jnp.bfloat16)
    grad_scale_qk = (grad_factor_query + grad_factor_key).reshape(-1)
    shard_query, shard_key, shard_value, shard_output, shard_up, shard_gate, shard_down = (
        lax.psum_scatter(
            grad_query.astype(jnp.bfloat16), "shards", scatter_dimension=0, tiled=True
        ).astype(jnp.float32),
        lax.psum_scatter(
            grad_key.astype(jnp.bfloat16), "shards", scatter_dimension=0, tiled=True
        ).astype(jnp.float32),
        lax.psum_scatter(
            grad_value.astype(jnp.bfloat16), "shards", scatter_dimension=0, tiled=True
        ).astype(jnp.float32),
        lax.psum_scatter(
            grad_output.astype(jnp.bfloat16), "shards", scatter_dimension=1, tiled=True
        ).astype(jnp.float32),
        lax.psum_scatter(
            grad_up.astype(jnp.bfloat16), "shards", scatter_dimension=0, tiled=True
        ).astype(jnp.float32),
        lax.psum_scatter(
            grad_gate.astype(jnp.bfloat16), "shards", scatter_dimension=0, tiled=True
        ).astype(jnp.float32),
        lax.psum_scatter(
            grad_down.astype(jnp.bfloat16), "shards", scatter_dimension=1, tiled=True
        ).astype(jnp.float32),
    )
    part_query, part_key, part_value, part_output, part_up, part_gate, part_down = (
        lax.psum_scatter(
            shard_query.astype(jnp.bfloat16), "context", scatter_dimension=0, tiled=True
        ).astype(jnp.float32),
        lax.psum_scatter(
            shard_key.astype(jnp.bfloat16), "context", scatter_dimension=0, tiled=True
        ).astype(jnp.float32),
        lax.psum_scatter(
            shard_value.astype(jnp.bfloat16), "context", scatter_dimension=0, tiled=True
        ).astype(jnp.float32),
        lax.psum_scatter(
            shard_output.astype(jnp.bfloat16), "context", scatter_dimension=1, tiled=True
        ).astype(jnp.float32),
        lax.psum_scatter(
            shard_up.astype(jnp.bfloat16), "context", scatter_dimension=0, tiled=True
        ).astype(jnp.float32),
        lax.psum_scatter(
            shard_gate.astype(jnp.bfloat16), "context", scatter_dimension=0, tiled=True
        ).astype(jnp.float32),
        lax.psum_scatter(
            shard_down.astype(jnp.bfloat16), "context", scatter_dimension=1, tiled=True
        ).astype(jnp.float32),
    )
    sum_query, sum_key, sum_value, sum_output, sum_up, sum_gate, sum_down = (
        lax.all_gather(part_query.astype(jnp.bfloat16), "context", axis=0, tiled=True).astype(
            part_query.dtype
        ),
        lax.all_gather(part_key.astype(jnp.bfloat16), "context", axis=0, tiled=True).astype(
            part_key.dtype
        ),
        lax.all_gather(part_value.astype(jnp.bfloat16), "context", axis=0, tiled=True).astype(
            part_value.dtype
        ),
        lax.all_gather(part_output.astype(jnp.bfloat16), "context", axis=1, tiled=True).astype(
            part_output.dtype
        ),
        lax.all_gather(part_up.astype(jnp.bfloat16), "context", axis=0, tiled=True).astype(
            part_up.dtype
        ),
        lax.all_gather(part_gate.astype(jnp.bfloat16), "context", axis=0, tiled=True).astype(
            part_gate.dtype
        ),
        lax.all_gather(part_down.astype(jnp.bfloat16), "context", axis=1, tiled=True).astype(
            part_down.dtype
        ),
    )
    total_scale_qk, total_alpha_attn, total_alpha_mlp, total_scale_up, total_scale_gate = lax.psum(
        (grad_scale_qk, grad_alpha_attn, grad_alpha_mlp, grad_scale_up, grad_scale_gate),
        ("shards", "context"),
    )
    return (
        block_low,
        grad_tokens,
        sum_query,
        sum_key,
        sum_value,
        sum_output,
        sum_up,
        sum_gate,
        sum_down,
        total_scale_qk,
        total_alpha_attn,
        total_alpha_mlp,
        total_scale_up,
        total_scale_gate,
    )


def solution(mesh):
    in_specs = (
        P(("shards", "context"), None),
        P(("shards", "context"), None),
        P(("shards", "context")),
        P(("shards", "context")),
        P("shards", "tensor"),
        P("shards", "tensor"),
        P("shards", "tensor"),
        P("tensor", "shards"),
        P("shards", "tensor"),
        P("shards", "tensor"),
        P("tensor", "shards"),
        P("tensor"),
        P(),
        P(),
        P("tensor"),
        P("tensor"),
    )
    out_specs = (
        P(("shards", "context"), None),
        P(("shards", "context"), None),
        P("shards", "tensor"),
        P("shards", "tensor"),
        P("shards", "tensor"),
        P("tensor", "shards"),
        P("shards", "tensor"),
        P("shards", "tensor"),
        P("tensor", "shards"),
        P("tensor"),
        P(),
        P(),
        P("tensor"),
        P("tensor"),
    )
    return jax.shard_map(
        on_device, mesh=mesh, in_specs=in_specs, out_specs=out_specs, check_vma=False
    )
```

profile of v0, /device:TPU:0, one launch (start us, length us, event | category | flops | bytes accessed | tf_op | source)
XLA Modules:
  0.0 1299.2 jit_solution(2730937836505166477)
XLA Ops:
  11.3 11.3 all_gather.48
  22.7 10.1 all_gather.49
  39.9 10.6 all_gather.50
  55.8 9.5 all_gather.51
  66.5 10.8 all_gather.52
  81.5 57.1 %while.28 = (s32[]{:T(128)}, bf16[5,1024,64]{1,2,0:T(8,128)(2,1)S(1)}, f32[5,1024]{1,0:T(8,128)S(1)}, bf16[5,1024,64]{2,1,0:T(8,128)(2,1)}, bf16[5,1536,64]{2,1,...) while((s32[]{:T(128)}, ...), condition=%wide.region_5.6_spmd.clone, body=%wide.region_2.5_spmd.clone.sunk | while | flops 421592064 | bytes 45289628 | solution.py:154
  140.0 9.3 all_gather.53
  156.1 188.1 %all-reduce.11.cloned.1.call-done = f32[1024,1280]{1,0:T(8,128)} async-done(((f32[1024,1280]{1,0:T(8,128)}), f32[1024,1280]{1,0:T(8,128)}) %all-reduce.11.cloned.1.call-update) | async-done | bytes 5242896 | tf_op jit(solution)/shard_map/psum | solution.py:157
  352.4 8.1 fusion.73
  360.6 8.7 multiply_convert_fusion.4
  369.3 8.7 fusion.74
  378.4 187.5 %all-reduce.13.cloned.1.call-done = f32[1024,1280]{1,0:T(8,128)} async-done(((f32[1024,1280]{1,0:T(8,128)}), f32[1024,1280]{1,0:T(8,128)}) %all-reduce.13.cloned.1.call-update) | async-done | bytes 5242896 | tf_op jit(solution)/shard_map/psum | solution.py:165
  581.1 9.5 multiply_reduce_fusion.1
  600.8 187.8 %all-reduce.15.cloned.1.call-done = f32[1024,1280]{1,0:T(8,128)} async-done(((f32[1024,1280]{1,0:T(8,128)}), f32[1024,1280]{1,0:T(8,128)}) %all-reduce.15.cloned.1.call-update) | async-done | bytes 5242896 | tf_op jit(solution)/shard_map/psum | solution.py:179
  788.5 9.5 multiply_reduce_fusion.3
  798.1 11.6 multiply_reduce_fusion.4
  814.4 68.5 %while.29 = (s32[]{:T(128)}, f32[5,1024,64]{1,2,0:T(8,128)}, f32[5,1536,64]{1,2,0:T(8,128)}, bf16[5,1536,64]{1,2,0:T(8,128)(2,1)}, bf16[5,1024,64]{2,1,0:T(8,128...) while((s32[]{:T(128)}, f32[5,1024,64]{1,2,0:T(8,128)}, ...), condition=%wide.region_19.20_spmd.clone, body=%wide.region_17.19_spmd.clone.sunk | while | flops 1027243008 | bytes 50515088 | solution.py:201
  909.2 7.5 convolution_convert_fusion.1
  945.7 40.9 %reduce-scatter.45.cloned.1.call-done = bf16[1280,320]{0,1:T(8,128)(2,1)} async-done(((bf16[1280,1280]{0,1:T(8,128)(2,1)}), bf16[1280,320]{0,1:T(8,128)(2,1)}) %reduce-scatter.45.cloned.1.call-update) | async-done | bytes 819216 | tf_op jit(solution)/shard_map/reduce_scatter | solution.py:261
  986.7 40.9 %reduce-scatter.37.cloned.1.call-done = bf16[320,1280]{1,0:T(8,128)(2,1)} async-done(((bf16[1280,1280]{1,0:T(8,128)(2,1)}), bf16[320,1280]{1,0:T(8,128)(2,1)}) %reduce-scatter.37.cloned.1.call-update) | async-done | bytes 819216 | tf_op jit(solution)/shard_map/reduce_scatter | solution.py:255
  1027.8 40.9 %reduce-scatter.41.cloned.1.call-done = bf16[320,1280]{1,0:T(8,128)(2,1)} async-done(((bf16[1280,1280]{1,0:T(8,128)(2,1)}), bf16[320,1280]{1,0:T(8,128)(2,1)}) %reduce-scatter.41.cloned.1.call-update) | async-done | bytes 819216 | tf_op jit(solution)/shard_map/reduce_scatter | solution.py:258
  1068.8 27.5 %reduce-scatter.57.cloned.1.call-done = bf16[320,320]{1,0:T(8,128)(2,1)} async-done(((bf16[1280,320]{1,0:T(8,128)(2,1)}), bf16[320,320]{1,0:T(8,128)(2,1)}) %reduce-scatter.57.cloned.1.call-update) | async-done | bytes 204816
  1096.3 27.3 %reduce-scatter.53.cloned.1.call-done = bf16[320,320]{1,0:T(8,128)(2,1)} async-done(((bf16[1280,320]{1,0:T(8,128)(2,1)}), bf16[320,320]{1,0:T(8,128)(2,1)}) %reduce-scatter.53.cloned.1.call-update) | async-done | bytes 204816
  1131.5 19.6 %reduce-scatter.49.cloned.1.call-done = bf16[320,320]{1,0:T(8,128)(2,1)} async-done(((bf16[1280,320]{1,0:T(8,128)(2,1)}), bf16[320,320]{1,0:T(8,128)(2,1)}) %reduce-scatter.49.cloned.1.call-update) | async-done | bytes 204816
  1151.3 7.1 add_convert_fusion.1
  1158.5 26.4 %all-reduce.5 = (f32[320]{0:T(512)}, f32[1280]{0:T(1024)}, f32[1280]{0:T(1024)}, f32[1280]{0:T(1024)}, f32[1280]{0:T(1024)}) all-reduce(f32[320]{0:T(512)S(1)} %add.196, f32[1280]{0:T(1024)S(1)} %copy-done.58, f32[1280]{0:T(1024)S(1)} %copy-done.57, ...), channel_id=1, replica_groups=mesh['shards'=4,'context'=2,'tensor'=4] {'shards','context'}, use_global_device_ids=true, to_apply=%region_41.42 | all-reduce | flops 5440 | bytes 43520 | tf_op jit(solution)/shard_map/psum | solution.py:311
  1191.6 19.3 %all_gather.63 = bf16[1280,320]{0,1:T(8,128)(2,1)S(1)} all-gather(bf16[1280,160]{0,1:T(8,128)(2,1)} %reduce-scatter.47.cloned.1.call-done), channel_id=1, replica_groups=mesh['shards'=4,'context'=2,'tensor'=4] {'context'}, dimensions={1}, use_global_device_ids=true | all-gather | bytes 1228800 | tf_op jit(solution)/shard_map/all_gather | solution.py:307
  1212.5 13.6 %all_gather.61 = bf16[320,1280]{1,0:T(8,128)(2,1)S(1)} all-gather(bf16[160,1280]{1,0:T(8,128)(2,1)} %reduce-scatter.39.cloned.1.call-done), channel_id=1, replica_groups=mesh['shards'=4,'context'=2,'tensor'=4] {'context'}, dimensions={0}, use_global_device_ids=true | all-gather | bytes 1228800 | tf_op jit(solution)/shard_map/all_gather | solution.py:301
  1227.3 7.2 reduce-scatter.43.cloned.1.call-done
  1234.5 13.6 %all_gather.62 = bf16[320,1280]{1,0:T(8,128)(2,1)S(1)} all-gather(bf16[160,1280]{1,0:T(8,128)(2,1)} %reduce-scatter.43.cloned.1.call-done), channel_id=1, replica_groups=mesh['shards'=4,'context'=2,'tensor'=4] {'context'}, dimensions={0}, use_global_device_ids=true | all-gather | bytes 1228800 | tf_op jit(solution)/shard_map/all_gather | solution.py:304
  1256.9 8.7 reduce-scatter.55.cloned.1.call-done
  1272.1 7.1 reduce-scatter.51.cloned.1.call-done
  (375 shorter events, 292.9 us)
Async XLA Ops:
  8.0 336.2 %all-reduce.11.cloned.1.call-start = ((), (), s32[]{:S(2)}) async-start(), calls=%async_computation.16 | async-start | bytes 10485760 | tf_op jit(solution)/shard_map/psum | solution.py:157
  138.6 15.6 %copy-start.36 = (bf16[5,1024,64]{1,2,0:T(8,128)(2,1)}, bf16[5,1024,64]{1,2,0:T(8,128)(2,1)S(1)}, u32[]{:S(2)}) copy-start(bf16[5,1024,64]{1,2,0:T(8,128)(2,1)S(1)} %get-tuple-element.106) | copy-start | bytes 1966084
  154.3 198.1 %all-gather.6.cloned.1.call-start = ((), (), s32[]{:S(2)}) async-start(), calls=%async_computation.18 | async-start | bytes 4096000 | tf_op jit(solution)/shard_map/all_gather | solution.py:95
  154.9 192.4 %copy-start.53 = (f32[1280]{0:T(1024)S(1)}, f32[1280]{0:T(1024)}, u32[]{:S(2)}) copy-start(f32[1280]{0:T(1024)} %param.32) | copy-start | bytes 15364
  154.9 205.7 %all-gather.4.cloned.1.call-start = ((), (), s32[]{:S(2)}) async-start(), calls=%async_computation.17 | async-start | bytes 4096000 | tf_op jit(solution)/shard_map/all_gather | solution.py:94
  155.5 213.8 %all-gather.8.cloned.1.call-start = ((), (), s32[]{:S(2)}) async-start(), calls=%async_computation.19 | async-start | bytes 4096000 | tf_op jit(solution)/shard_map/all_gather | solution.py:96
  156.0 410.0 %all-reduce.13.cloned.1.call-start = ((), (), s32[]{:S(2)}) async-start(), calls=%async_computation.20 | async-start | bytes 10485760 | tf_op jit(solution)/shard_map/psum | solution.py:165
  378.0 191.1 %copy-start.4 = (bf16[1024,1280]{1,0:T(8,128)(2,1)S(1)}, bf16[1024,1280]{1,0:T(8,128)(2,1)}, u32[]{:S(2)}) copy-start(bf16[1024,1280]{1,0:T(8,128)(2,1)} %param.21) | copy-start | bytes 7864324
  378.0 191.1 %copy-start.52 = (f32[1280]{0:T(1024)S(1)}, f32[1280]{0:T(1024)}, u32[]{:S(2)}) copy-start(f32[1280]{0:T(1024)} %param.33) | copy-start | bytes 15364
  378.0 410.5 %all-reduce.15.cloned.1.call-start = ((), (), s32[]{:S(2)}) async-start(), calls=%async_computation.21 | async-start | bytes 10485760 | tf_op jit(solution)/shard_map/psum | solution.py:179
  600.5 319.1 %reduce-scatter.33.cloned.1.call-start = ((), (), s32[]{:S(2)}) async-start(), calls=%async_computation.22 | async-start | bytes 983040 | tf_op jit(solution)/shard_map/reduce_scatter | solution.py:207
  885.3 36.2 %reduce-scatter.35.cloned.1.call-start = ((), (), s32[]{:S(2)}) async-start(), calls=%async_computation.23 | async-start | bytes 983040 | tf_op jit(solution)/shard_map/reduce_scatter | solution.py:213
  887.4 58.2 %reduce-scatter.61.cloned.1.call-start = ((), (), s32[]{:S(2)}) async-start(), calls=%async_computation.37 | async-start | bytes 1228800
  893.7 93.0 %reduce-scatter.45.cloned.1.call-start = ((), (), s32[]{:S(2)}) async-start(), calls=%async_computation.29 | async-start | bytes 4096000 | tf_op jit(solution)/shard_map/reduce_scatter | solution.py:261
  900.6 127.1 %reduce-scatter.37.cloned.1.call-start = ((), (), s32[]{:S(2)}) async-start(), calls=%async_computation.25 | async-start | bytes 4096000 | tf_op jit(solution)/shard_map/reduce_scatter | solution.py:255
  909.1 159.6 %reduce-scatter.41.cloned.1.call-start = ((), (), s32[]{:S(2)}) async-start(), calls=%async_computation.27 | async-start | bytes 4096000 | tf_op jit(solution)/shard_map/reduce_scatter | solution.py:258
  916.7 179.5 %reduce-scatter.57.cloned.1.call-start = ((), (), s32[]{:S(2)}) async-start(), calls=%async_computation.35 | async-start | bytes 1228800
  927.8 195.8 %reduce-scatter.53.cloned.1.call-start = ((), (), s32[]{:S(2)}) async-start(), calls=%async_computation.33 | async-start | bytes 1228800
  937.8 213.3 %reduce-scatter.49.cloned.1.call-start = ((), (), s32[]{:S(2)}) async-start(), calls=%async_computation.31 | async-start | bytes 1228800
  942.3 181.5 %copy-start.27 = (bf16[1280,320]{1,0:T(8,128)(2,1)S(1)}, bf16[1280,320]{1,0:T(8,128)(2,1)}, u32[]{:S(2)}) copy-start(bf16[1280,320]{1,0:T(8,128)(2,1)} %copy-done.26) | copy-start | bytes 2457604
  944.6 240.3 %reduce-scatter.63.cloned.1.call-start = ((), (), s32[]{:S(2)}) async-start(), calls=%async_computation.38 | async-start | bytes 368640
  945.7 245.9 %reduce-scatter.47.cloned.1.call-start = ((), (), s32[]{:S(2)}) async-start(), calls=%async_computation.30 | async-start | bytes 1228800 | tf_op jit(solution)/shard_map/reduce_scatter | solution.py:284
  986.7 225.8 %reduce-scatter.39.cloned.1.call-start = ((), (), s32[]{:S(2)}) async-start(), calls=%async_computation.26 | async-start | bytes 1228800 | tf_op jit(solution)/shard_map/reduce_scatter | solution.py:278
  1027.7 206.8 %reduce-scatter.43.cloned.1.call-start = ((), (), s32[]{:S(2)}) async-start(), calls=%async_computation.28 | async-start | bytes 1228800 | tf_op jit(solution)/shard_map/reduce_scatter | solution.py:281
  1068.7 181.4 %reduce-scatter.59.cloned.1.call-start = ((), (), s32[]{:S(2)}) async-start(), calls=%async_computation.36 | async-start | bytes 368640 | tf_op jit(solution)/shard_map/reduce_scatter | solution.py:272
  1096.3 169.3 %reduce-scatter.55.cloned.1.call-start = ((), (), s32[]{:S(2)}) async-start(), calls=%async_computation.34 | async-start | bytes 368640 | tf_op jit(solution)/shard_map/reduce_scatter | solution.py:269
  1123.7 155.5 %reduce-scatter.51.cloned.1.call-start = ((), (), s32[]{:S(2)}) async-start(), calls=%async_computation.32 | async-start | bytes 368640 | tf_op jit(solution)/shard_map/reduce_scatter | solution.py:266
  1127.7 23.6 %copy-start.23 = (bf16[1280,320]{1,0:T(8,128)(2,1)S(1)}, bf16[1280,320]{1,0:T(8,128)(2,1)}, u32[]{:S(2)}) copy-start(bf16[1280,320]{1,0:T(8,128)(2,1)} %copy-done.22) | copy-start | bytes 2457604
  1127.7 23.6 %copy-start.38 = (bf16[512,5,64]{0,2,1:T(8,128)(2,1)S(1)}, bf16[512,5,64]{0,2,1:T(8,128)(2,1)}, u32[]{:S(2)}) copy-start(bf16[512,5,64]{0,2,1:T(8,128)(2,1)} %slice.82) | copy-start | bytes 983044
  1127.7 23.6 %copy-start.47 = (bf16[512,320]{0,1:T(8,128)(2,1)S(1)}, bf16[512,320]{0,1:T(8,128)(2,1)}, u32[]{:S(2)}) copy-start(bf16[512,320]{0,1:T(8,128)(2,1)} %reduce-scatter.35.cloned.1.call-done) | copy-start | bytes 983044
  1151.2 134.5 %all-reduce.17.cloned.1.call-start = ((), (), s32[]{:S(2)}) async-start(), calls=%async_computation.24 | async-start | bytes 5242880 | tf_op jit(solution)/shard_map/psum | solution.py:239
  1227.3 58.4 %copy-start.54 = (f32[1280]{0:T(1024)S(1)}, f32[1280]{0:T(1024)}, u32[]{:S(2)}) copy-start(f32[1280]{0:T(1024)} %param.32) | copy-start | bytes 15364
  (74 other events, 398.5 us)
Sparse Core Ops, SparseCore 0:
  154.4 189.7 all-reduce.10
  378.1 187.8 all-reduce.12
  600.6 187.8 all-reduce.14
  1158.6 104.0 all-reduce.16
Sparse Core Ops, SparseCore 1:
  156.3 29.9 all-gather.5
  187.7 29.1 all-gather.3
  218.3 29.1 all-gather.7
  885.4 14.9 reduce-scatter.32
  902.6 16.0 reduce-scatter.34
  921.3 24.3 reduce-scatter.60
  948.1 38.5 reduce-scatter.44
  989.1 38.5 reduce-scatter.36
  1030.1 38.5 reduce-scatter.40
  1071.9 24.3 reduce-scatter.56
  1099.3 24.3 reduce-scatter.52
  1126.8 24.3 reduce-scatter.48
  1153.3 11.8 reduce-scatter.62
  1167.4 18.7 reduce-scatter.46
  1188.4 24.0 reduce-scatter.38
  1214.7 19.7 reduce-scatter.42
  1236.8 13.3 reduce-scatter.58
  1252.4 13.1 reduce-scatter.54
  1267.6 11.5 reduce-scatter.50
where the time goes:
time: 1310 us; the launch traced here: 1300 us
  waiting for transfers between devices  788 us (60%)
  matrix products  205 us (16%)
  blocking collectives  158 us (12%)
  other arithmetic  74.7 us (6%)
  local copies, waits for them, and re-layouts  54.5 us (4%)
  between operations  17.3 us (1%)
    psum x1, waiting for transfers between devices, on_device(): attn_out = lax.psum(attn_terms, 'tensor')  188 us
    psum x1, waiting for transfers between devices, on_device(): grad_after = grad_after + lax.psum(input_terms, 'tensor')  188 us
    psum x1, waiting for transfers between devices, on_device(): merged = lax.psum(merged_terms, 'tensor')  188 us
    unnamed x28, waiting for transfers between devices  77.3 us
    dot_general x17, matrix products, outer_sum(): lax.dot_general(left, right, (((0,), (0,)), ((), ())), preferred_element_...  51.7 us
    reduce_scatter x1, waiting for transfers between devices, on_device(): lax.psum_scatter(grad_gate.astype(jnp.bfloat16), 'shards', scatter_dimens...  40.9 us
    reduce_scatter x1, waiting for transfers between devices, on_device(): lax.psum_scatter(grad_down.astype(jnp.bfloat16), 'shards', scatter_dimens...  40.9 us
    reduce_scatter x1, waiting for transfers between devices, on_device(): lax.psum_scatter(grad_up.astype(jnp.bfloat16), 'shards', scatter_dimensio...  40.9 us
  transfers between devices with their start and end apart: 23, of which 15 were waited for; matrix products, arithmetic and copies ran while one was open for 8% of the time, Pallas kernels for 0%

commit v1 on v0

--- a/solution.py
+++ b/solution.py
@@ -162,7 +162,7 @@
     inner, swiglu_back = jax.vjp(swiglu, up_proj, gate_proj, scale_up, scale_gate)
     inner_low = inner.astype(jnp.bfloat16)
     merged_terms = jnp.dot(inner_low, full_down, preferred_element_type=jnp.float32)
-    merged = lax.psum(merged_terms, "tensor")
+    merged = jnp.sum(lax.all_gather(merged_terms, "tensor"), axis=0)
     block_whole, out_back = jax.vjp(residual_step, after_attn, merged, alpha_mlp)
     block_low = block_whole.astype(jnp.bfloat16)
     grad_after, grad_merged, grad_alpha_mlp = out_back(cotangent.astype(jnp.float32))

time: 1310 us -> 1490 us (1.14)
  waiting for transfers between devices: 788 us -> 956 us
    all_gather x0 -> x1, waiting for transfers between devices: none -> 355 us  [on_device(): merged = jnp.sum(lax.all_gather(merged_terms, 'tensor'), axis=0)]
    psum x1 -> x0, waiting for transfers between devices: 188 us -> none  [on_device(): merged = lax.psum(merged_terms, 'tensor')]
  transfers between devices with their start and end apart: 23 -> 23, of which waited for: 15 -> 15; matrix products, arithmetic and copies ran while one was open for 8% -> 7% of each run, Pallas kernels for 0% -> 0%
where the time goes in v1:
time: 1490 us; the launch traced here: 1480 us
  waiting for transfers between devices  956 us (64%)
  matrix products  205 us (14%)
  blocking collectives  157 us (11%)
  other arithmetic  85.4 us (6%)
  local copies, waits for them, and re-layouts  54.6 us (4%)
  between operations  17.2 us (1%)
    all_gather x1, waiting for transfers between devices, on_device(): merged = jnp.sum(lax.all_gather(merged_terms, 'tensor'), axis=0)  355 us
    psum x1, waiting for transfers between devices, on_device(): attn_out = lax.psum(attn_terms, 'tensor')  188 us
    psum x1, waiting for transfers between devices, on_device(): grad_after = grad_after + lax.psum(input_terms, 'tensor')  187 us
    unnamed x28, waiting for transfers between devices  77.3 us
    dot_general x17, matrix products, outer_sum(): lax.dot_general(left, right, (((0,), (0,)), ((), ())), preferred_element_...  51.7 us
    reduce_scatter x1, waiting for transfers between devices, on_device(): lax.psum_scatter(grad_gate.astype(jnp.bfloat16), 'shards', scatter_dimens...  41 us
    reduce_scatter x1, waiting for transfers between devices, on_device(): lax.psum_scatter(grad_down.astype(jnp.bfloat16), 'shards', scatter_dimens...  40.9 us
    reduce_scatter x1, waiting for transfers between devices, on_device(): lax.psum_scatter(grad_up.astype(jnp.bfloat16), 'shards', scatter_dimensio...  40.9 us
  transfers between devices with their start and end apart: 23, of which 15 were waited for; matrix products, arithmetic and copies ran while one was open for 7% of the time, Pallas kernels for 0%

profile of v1, /device:TPU:0, one launch (start us, length us, event | category | flops | bytes accessed | tf_op | source)
XLA Modules:
  0.0 1477.5 jit_solution(2544227415093545300)
XLA Ops:
  11.3 11.3 all_gather.54
  22.7 10.1 all_gather.55
  40.0 10.6 all_gather.56
  55.9 9.5 all_gather.57
  66.5 10.8 all_gather.58
  81.6 57.1 %while.28 = (s32[]{:T(128)}, bf16[5,1024,64]{1,2,0:T(8,128)(2,1)S(1)}, f32[5,1024]{1,0:T(8,128)S(1)}, bf16[5,1024,64]{2,1,0:T(8,128)(2,1)}, bf16[5,1536,64]{2,1,...) while((s32[]{:T(128)}, ...), condition=%wide.region_5.6_spmd.clone, body=%wide.region_2.5_spmd.clone.sunk | while | flops 421592064 | bytes 45289628 | solution.py:154
  140.1 9.3 all_gather.59
  156.1 188.1 %all-reduce.10.cloned.1.call-done = f32[1024,1280]{1,0:T(8,128)} async-done(((f32[1024,1280]{1,0:T(8,128)}), f32[1024,1280]{1,0:T(8,128)}) %all-reduce.10.cloned.1.call-update) | async-done | bytes 5242896 | tf_op jit(solution)/shard_map/psum | solution.py:157
  352.5 8.1 fusion.73
  360.7 8.7 multiply_convert_fusion.4
  369.3 8.7 fusion.74
  378.5 355.5 %all-gather.12.cloned.1.call-done = f32[4096,1280]{1,0:T(8,128)} async-done(((f32[1024,1280]{1,0:T(8,128)}), f32[4096,1280]{1,0:T(8,128)}) %all-gather.12.cloned.1.call-update) | async-done | bytes 20971536 | tf_op jit(solution)/shard_map/all_gather | solution.py:165
  734.0 11.0 reduce_sum.192
  759.8 9.5 multiply_reduce_fusion.1
  779.5 187.4 %all-reduce.12.cloned.1.call-done = f32[1024,1280]{1,0:T(8,128)} async-done(((f32[1024,1280]{1,0:T(8,128)}), f32[1024,1280]{1,0:T(8,128)}) %all-reduce.12.cloned.1.call-update) | async-done | bytes 5242896 | tf_op jit(solution)/shard_map/psum | solution.py:179
  966.8 9.5 multiply_reduce_fusion.3
  976.4 11.6 multiply_reduce_fusion.4
  992.7 68.5 %while.29 = (s32[]{:T(128)}, f32[5,1024,64]{1,2,0:T(8,128)}, f32[5,1536,64]{1,2,0:T(8,128)}, bf16[5,1536,64]{1,2,0:T(8,128)(2,1)}, bf16[5,1024,64]{2,1,0:T(8,128...) while((s32[]{:T(128)}, f32[5,1024,64]{1,2,0:T(8,128)}, ...), condition=%wide.region_19.20_spmd.clone, body=%wide.region_17.19_spmd.clone.sunk | while | flops 1027243008 | bytes 50515088 | solution.py:201
  1087.4 7.5 convolution_convert_fusion.1
  1124.0 40.9 %reduce-scatter.45.cloned.1.call-done = bf16[1280,320]{0,1:T(8,128)(2,1)} async-done(((bf16[1280,1280]{0,1:T(8,128)(2,1)}), bf16[1280,320]{0,1:T(8,128)(2,1)}) %reduce-scatter.45.cloned.1.call-update) | async-done | bytes 819216 | tf_op jit(solution)/shard_map/reduce_scatter | solution.py:261
  1165.0 40.9 %reduce-scatter.37.cloned.1.call-done = bf16[320,1280]{1,0:T(8,128)(2,1)} async-done(((bf16[1280,1280]{1,0:T(8,128)(2,1)}), bf16[320,1280]{1,0:T(8,128)(2,1)}) %reduce-scatter.37.cloned.1.call-update) | async-done | bytes 819216 | tf_op jit(solution)/shard_map/reduce_scatter | solution.py:255
  1206.0 41.0 %reduce-scatter.41.cloned.1.call-done = bf16[320,1280]{1,0:T(8,128)(2,1)} async-done(((bf16[1280,1280]{1,0:T(8,128)(2,1)}), bf16[320,1280]{1,0:T(8,128)(2,1)}) %reduce-scatter.41.cloned.1.call-update) | async-done | bytes 819216 | tf_op jit(solution)/shard_map/reduce_scatter | solution.py:258
  1247.0 27.5 %reduce-scatter.57.cloned.1.call-done = bf16[320,320]{1,0:T(8,128)(2,1)} async-done(((bf16[1280,320]{1,0:T(8,128)(2,1)}), bf16[320,320]{1,0:T(8,128)(2,1)}) %reduce-scatter.57.cloned.1.call-update) | async-done | bytes 204816
  1274.5 27.3 %reduce-scatter.53.cloned.1.call-done = bf16[320,320]{1,0:T(8,128)(2,1)} async-done(((bf16[1280,320]{1,0:T(8,128)(2,1)}), bf16[320,320]{1,0:T(8,128)(2,1)}) %reduce-scatter.53.cloned.1.call-update) | async-done | bytes 204816
  1309.8 19.6 %reduce-scatter.49.cloned.1.call-done = bf16[320,320]{1,0:T(8,128)(2,1)} async-done(((bf16[1280,320]{1,0:T(8,128)(2,1)}), bf16[320,320]{1,0:T(8,128)(2,1)}) %reduce-scatter.49.cloned.1.call-update) | async-done | bytes 204816
  1329.5 7.1 add_convert_fusion.1
  1336.8 26.4 %all-reduce.5 = (f32[320]{0:T(512)}, f32[1280]{0:T(1024)}, f32[1280]{0:T(1024)}, f32[1280]{0:T(1024)}, f32[1280]{0:T(1024)}) all-reduce(f32[320]{0:T(512)S(1)} %add.194, f32[1280]{0:T(1024)S(1)} %copy-done.58, f32[1280]{0:T(1024)S(1)} %copy-done.57, ...), channel_id=1, replica_groups=mesh['shards'=4,'context'=2,'tensor'=4] {'shards','context'}, use_global_device_ids=true, to_apply=%region_41.42 | all-reduce | flops 5440 | bytes 43520 | tf_op jit(solution)/shard_map/psum | solution.py:311
  1369.9 19.3 %all_gather.71 = bf16[1280,320]{0,1:T(8,128)(2,1)S(1)} all-gather(bf16[1280,160]{0,1:T(8,128)(2,1)} %reduce-scatter.47.cloned.1.call-done), channel_id=1, replica_groups=mesh['shards'=4,'context'=2,'tensor'=4] {'context'}, dimensions={1}, use_global_device_ids=true | all-gather | bytes 1228800 | tf_op jit(solution)/shard_map/all_gather | solution.py:307
  1390.7 13.3 all_gather.69
  1405.3 7.4 reduce-scatter.43.cloned.1.call-done
  1412.7 13.4 all_gather.70
  1435.2 8.6 reduce-scatter.55.cloned.1.call-done
  (376 shorter events, 300.0 us)
Async XLA Ops:
  8.0 336.2 %all-reduce.10.cloned.1.call-start = ((), (), s32[]{:S(2)}) async-start(), calls=%async_computation.16 | async-start | bytes 10485760 | tf_op jit(solution)/shard_map/psum | solution.py:157
  66.5 15.1 %copy-start.35 = (bf16[5,1024,64]{1,2,0:T(8,128)(2,1)S(1)}, bf16[5,1024,64]{1,2,0:T(8,128)(2,1)}, u32[]{:S(2)}) copy-start(bf16[5,1024,64]{1,2,0:T(8,128)(2,1)} %custom-call) | copy-start | bytes 1966084
  66.5 15.1 %copy-start.59 = (s32[1024]{0:T(1024)S(1)}, s32[1024]{0:T(1024)}, u32[]{:S(2)}) copy-start(s32[1024]{0:T(1024)} %param.23) | copy-start | bytes 12292
  138.7 15.6 %copy-start.36 = (bf16[5,1024,64]{1,2,0:T(8,128)(2,1)}, bf16[5,1024,64]{1,2,0:T(8,128)(2,1)S(1)}, u32[]{:S(2)}) copy-start(bf16[5,1024,64]{1,2,0:T(8,128)(2,1)S(1)} %get-tuple-element.106) | copy-start | bytes 1966084
  154.3 198.2 %all-gather.8.cloned.1.call-start = ((), (), s32[]{:S(2)}) async-start(), calls=%async_computation.18 | async-start | bytes 4096000 | tf_op jit(solution)/shard_map/all_gather | solution.py:95
  154.9 192.4 %copy-start.53 = (f32[1280]{0:T(1024)S(1)}, f32[1280]{0:T(1024)}, u32[]{:S(2)}) copy-start(f32[1280]{0:T(1024)} %param.32) | copy-start | bytes 15364
  154.9 205.7 %all-gather.6.cloned.1.call-start = ((), (), s32[]{:S(2)}) async-start(), calls=%async_computation.17 | async-start | bytes 4096000 | tf_op jit(solution)/shard_map/all_gather | solution.py:94
  155.5 213.8 %all-gather.10.cloned.1.call-start = ((), (), s32[]{:S(2)}) async-start(), calls=%async_computation.19 | async-start | bytes 4096000 | tf_op jit(solution)/shard_map/all_gather | solution.py:96
  156.1 577.9 %all-gather.12.cloned.1.call-start = ((), (), s32[]{:S(2)}) async-start(), calls=%async_computation.30 | async-start | bytes 26214400 | tf_op jit(solution)/shard_map/all_gather | solution.py:165
  378.0 588.8 %all-reduce.12.cloned.1.call-start = ((), (), s32[]{:S(2)}) async-start(), calls=%async_computation.20 | async-start | bytes 10485760 | tf_op jit(solution)/shard_map/psum | solution.py:179
  779.2 318.7 %reduce-scatter.33.cloned.1.call-start = ((), (), s32[]{:S(2)}) async-start(), calls=%async_computation.21 | async-start | bytes 983040 | tf_op jit(solution)/shard_map/reduce_scatter | solution.py:207
  1063.6 36.2 %reduce-scatter.35.cloned.1.call-start = ((), (), s32[]{:S(2)}) async-start(), calls=%async_computation.22 | async-start | bytes 983040 | tf_op jit(solution)/shard_map/reduce_scatter | solution.py:213
  1065.7 58.2 %reduce-scatter.61.cloned.1.call-start = ((), (), s32[]{:S(2)}) async-start(), calls=%async_computation.37 | async-start | bytes 1228800
  1072.0 93.0 %reduce-scatter.45.cloned.1.call-start = ((), (), s32[]{:S(2)}) async-start(), calls=%async_computation.28 | async-start | bytes 4096000 | tf_op jit(solution)/shard_map/reduce_scatter | solution.py:261
  1078.9 127.0 %reduce-scatter.37.cloned.1.call-start = ((), (), s32[]{:S(2)}) async-start(), calls=%async_computation.24 | async-start | bytes 4096000 | tf_op jit(solution)/shard_map/reduce_scatter | solution.py:255
  1087.3 159.6 %reduce-scatter.41.cloned.1.call-start = ((), (), s32[]{:S(2)}) async-start(), calls=%async_computation.26 | async-start | bytes 4096000 | tf_op jit(solution)/shard_map/reduce_scatter | solution.py:258
  1095.0 179.5 %reduce-scatter.57.cloned.1.call-start = ((), (), s32[]{:S(2)}) async-start(), calls=%async_computation.35 | async-start | bytes 1228800
  1106.1 195.8 %reduce-scatter.53.cloned.1.call-start = ((), (), s32[]{:S(2)}) async-start(), calls=%async_computation.33 | async-start | bytes 1228800
  1116.1 213.3 %reduce-scatter.49.cloned.1.call-start = ((), (), s32[]{:S(2)}) async-start(), calls=%async_computation.31 | async-start | bytes 1228800
  1120.5 181.4 %copy-start.27 = (bf16[1280,320]{1,0:T(8,128)(2,1)S(1)}, bf16[1280,320]{1,0:T(8,128)(2,1)}, u32[]{:S(2)}) copy-start(bf16[1280,320]{1,0:T(8,128)(2,1)} %copy-done.26) | copy-start | bytes 2457604
  1122.8 240.3 %reduce-scatter.63.cloned.1.call-start = ((), (), s32[]{:S(2)}) async-start(), calls=%async_computation.38 | async-start | bytes 368640
  1123.9 245.9 %reduce-scatter.47.cloned.1.call-start = ((), (), s32[]{:S(2)}) async-start(), calls=%async_computation.29 | async-start | bytes 1228800 | tf_op jit(solution)/shard_map/reduce_scatter | solution.py:284
  1164.9 225.8 %reduce-scatter.39.cloned.1.call-start = ((), (), s32[]{:S(2)}) async-start(), calls=%async_computation.25 | async-start | bytes 1228800 | tf_op jit(solution)/shard_map/reduce_scatter | solution.py:278
  1205.9 206.8 %reduce-scatter.43.cloned.1.call-start = ((), (), s32[]{:S(2)}) async-start(), calls=%async_computation.27 | async-start | bytes 1228800 | tf_op jit(solution)/shard_map/reduce_scatter | solution.py:281
  1247.0 181.4 %reduce-scatter.59.cloned.1.call-start = ((), (), s32[]{:S(2)}) async-start(), calls=%async_computation.36 | async-start | bytes 368640 | tf_op jit(solution)/shard_map/reduce_scatter | solution.py:272
  1274.5 169.3 %reduce-scatter.55.cloned.1.call-start = ((), (), s32[]{:S(2)}) async-start(), calls=%async_computation.34 | async-start | bytes 368640 | tf_op jit(solution)/shard_map/reduce_scatter | solution.py:269
  1301.9 155.5 %reduce-scatter.51.cloned.1.call-start = ((), (), s32[]{:S(2)}) async-start(), calls=%async_computation.32 | async-start | bytes 368640 | tf_op jit(solution)/shard_map/reduce_scatter | solution.py:266
  1305.9 23.6 %copy-start.23 = (bf16[1280,320]{1,0:T(8,128)(2,1)S(1)}, bf16[1280,320]{1,0:T(8,128)(2,1)}, u32[]{:S(2)}) copy-start(bf16[1280,320]{1,0:T(8,128)(2,1)} %copy-done.22) | copy-start | bytes 2457604
  1305.9 23.6 %copy-start.38 = (bf16[512,5,64]{0,2,1:T(8,128)(2,1)S(1)}, bf16[512,5,64]{0,2,1:T(8,128)(2,1)}, u32[]{:S(2)}) copy-start(bf16[512,5,64]{0,2,1:T(8,128)(2,1)} %slice.82) | copy-start | bytes 983044
  1305.9 23.6 %copy-start.47 = (bf16[512,320]{0,1:T(8,128)(2,1)S(1)}, bf16[512,320]{0,1:T(8,128)(2,1)}, u32[]{:S(2)}) copy-start(bf16[512,320]{0,1:T(8,128)(2,1)} %reduce-scatter.35.cloned.1.call-done) | copy-start | bytes 983044
  1329.5 134.5 %all-reduce.14.cloned.1.call-start = ((), (), s32[]{:S(2)}) async-start(), calls=%async_computation.23 | async-start | bytes 5242880 | tf_op jit(solution)/shard_map/psum | solution.py:239
  1405.3 58.6 %copy-start.54 = (f32[1280]{0:T(1024)S(1)}, f32[1280]{0:T(1024)}, u32[]{:S(2)}) copy-start(f32[1280]{0:T(1024)} %param.32) | copy-start | bytes 15364
  (74 other events, 386.1 us)
Sparse Core Ops, SparseCore 0:
  154.4 189.7 all-reduce.9
  378.2 355.7 all-gather.11
  779.3 187.4 all-reduce.11
  1336.8 104.0 all-reduce.13
Sparse Core Ops, SparseCore 1:
  156.4 29.9 all-gather.7
  187.8 29.1 all-gather.5
  218.4 29.1 all-gather.9
  1063.7 14.9 reduce-scatter.32
  1080.9 16.0 reduce-scatter.34
  1099.5 24.3 reduce-scatter.60
  1126.3 38.5 reduce-scatter.44
  1167.3 38.5 reduce-scatter.36
  1208.3 38.5 reduce-scatter.40
  1250.1 24.3 reduce-scatter.56
  1277.5 24.3 reduce-scatter.52
  1305.0 24.3 reduce-scatter.48
  1331.5 11.8 reduce-scatter.62
  1345.7 18.7 reduce-scatter.46
  1366.7 24.0 reduce-scatter.38
  1393.0 19.7 reduce-scatter.42
  1415.0 13.4 reduce-scatter.58
  1430.7 13.0 reduce-scatter.54
  1445.9 11.5 reduce-scatter.50
